TPU v7x, 32 devices: a whole 2x2x4 slice. The times are simulated.
32 devices in a mesh: dp: 16 (over z, y, x), mp: 2 (over core).
Axes of the slice: x: 2, y: 2, z: 4, core: 2. Of those that a mesh axis runs over, the one named last changes fastest.
Arguments:
- gradient: bfloat16 [2, 8, 512, 512], P('mp', None, 'dp'), may hold values from -54 to 54
- owners: int32 [2, 8], P('mp'), may hold values from 0 to 15, as said below
- left_stats: float32 [2, 16, 512, 512], P('mp', 'dp'), may hold values from -0.2 to 20.2
- right_stats: float32 [2, 16, 512, 512], P('mp', 'dp'), may hold values from -0.2 to 20.2
- left_roots_old: bfloat16 [2, 16, 512, 512], P('mp', 'dp'), may hold values from -0.1 to 1.5
- right_roots_old: bfloat16 [2, 16, 512, 512], P('mp', 'dp'), may hold values from -0.1 to 1.5
Outputs:
- update: bfloat16 [2, 8, 512, 512], P('mp', None, 'dp')
- left_roots: bfloat16 [2, 16, 512, 512], P('mp', 'dp')
- right_roots: bfloat16 [2, 16, 512, 512], P('mp', 'dp')
Inputs may be any that keep to these rules, and one draw needn't show every extreme that they name: In each row the 8 owners are distinct. Owner o holds a block of row m exactly when owner (o + 8) mod 16 of row m holds none, and exactly when owner o of row (m + 1) mod 2 holds none.
All inputs are finite; a program needn't handle non-finite values.
Results may differ from a plain program's by a relative error of at most 0.0067.
Values may be sent and summed in bfloat16 or wider, within the bound.
A program may use at most 64 MiB of HBM per device.

v0:
```python
import jax
import jax.numpy as jnp
from jax import lax
from jax.sharding import PartitionSpec as P

ITERS = 2


stat_decay = 0.9
ridge_term = 0.001
tiny_term = 1e-06


def newton_root(statistic):
    dimension = statistic.shape[0]
    identity = jnp.eye(dimension, dtype=jnp.float32)
    shifted = statistic + ridge_term * identity
    norm_scale = jnp.sqrt(jnp.sum(shifted * shifted) + tiny_term)
    matrix = shifted / norm_scale
    iterate = identity
    for iteration in range(ITERS):
        factor = ((5.0 * identity - matrix) / 4.0).astype(jnp.bfloat16)
        if iteration == 0:
            iterate = norm_scale ** (-0.25) * lax.optimization_barrier(factor).astype(jnp.float32)
        else:
            iterate = jnp.dot(
                iterate.astype(jnp.bfloat16), factor, preferred_element_type=jnp.float32
            )
        if iteration + 1 < ITERS:
            factor_two = jnp.dot(factor, factor, preferred_element_type=jnp.float32).astype(
                jnp.bfloat16
            )
            factor_four = jnp.dot(
                factor_two, factor_two, preferred_element_type=jnp.float32
            ).astype(jnp.bfloat16)
            matrix = jnp.dot(
                factor_four, matrix.astype(jnp.bfloat16), preferred_element_type=jnp.float32
            )
    return iterate.astype(jnp.bfloat16)


def shards(gradient, owners, left_stats, right_stats, left_roots_old, right_roots_old):
    dp_count = lax.axis_size("dp")
    my_index = lax.axis_index("dp")
    blocks_here = gradient.shape[1]
    row_count = gradient.shape[2]
    block_width = gradient.shape[3]
    owner_table = owners[0]
    owner_ids = jnp.arange(dp_count, dtype=jnp.int32)
    selector = (owner_table[None, :] == owner_ids[:, None]).astype(jnp.bfloat16)
    flat_grad = gradient[0].reshape(blocks_here, row_count * block_width)
    outgoing = jnp.dot(selector, flat_grad, preferred_element_type=jnp.float32).astype(jnp.bfloat16)
    outgoing = outgoing.reshape(dp_count, row_count, block_width)
    arrived = lax.all_to_all(outgoing, "dp", split_axis=0, concat_axis=1, tiled=True)
    grad_block = arrived[0]
    is_mine = owner_table == my_index
    mine_weight = is_mine.astype(jnp.float32)
    is_busy = jnp.any(is_mine)
    left_gram = jnp.einsum("ik,jk->ij", grad_block, grad_block, preferred_element_type=jnp.float32)
    right_gram = jnp.einsum("ki,kj->ij", grad_block, grad_block, preferred_element_type=jnp.float32)
    left_new = stat_decay * left_stats[0, 0] + left_gram / block_width
    right_new = stat_decay * right_stats[0, 0] + right_gram / block_width
    shaded = jnp.dot(grad_block, right_roots_old[0, 0], preferred_element_type=jnp.float32).astype(
        jnp.bfloat16
    )
    direction = jnp.dot(left_roots_old[0, 0], shaded, preferred_element_type=jnp.float32).astype(
        jnp.bfloat16
    )
    squares = jnp.stack(
        [
            jnp.sum(jnp.square(grad_block.astype(jnp.float32))),
            jnp.sum(jnp.square(direction.astype(jnp.float32))),
        ]
    )
    graft_terms = squares[:, None] * mine_weight[None, :]
    returned = lax.all_to_all(direction[None], "dp", split_axis=1, concat_axis=0, tiled=True)
    totals = lax.psum(graft_terms, ("dp", "mp"))
    graft_scale = jnp.sqrt(totals[0] / (totals[1] + tiny_term))
    pieces = jnp.einsum(
        "on,or->nr",
        selector,
        returned.reshape(dp_count, row_count * block_width),
        preferred_element_type=jnp.float32,
    )
    update = (
        (graft_scale[:, None] * pieces)
        .astype(jnp.bfloat16)
        .reshape(1, blocks_here, row_count, block_width)
    )
    zero_root = jnp.zeros((block_width, block_width), jnp.bfloat16)
    left_root, right_root = lax.cond(
        is_busy,
        lambda: (newton_root(left_new), newton_root(right_new)),
        lambda: (zero_root, zero_root),
    )
    return (update, left_root[None, None], right_root[None, None])


def solution(mesh):
    return jax.shard_map(
        shards,
        mesh=mesh,
        in_specs=(
            P("mp", None, "dp", None),
            P("mp", None),
            P("mp", "dp", None, None),
            P("mp", "dp", None, None),
            P("mp", "dp", None, None),
            P("mp", "dp", None, None),
        ),
        out_specs=(P("mp", None, "dp", None), P("mp", "dp", None, None), P("mp", "dp", None, None)),
        check_vma=False,
    )
```

profile of v0, /device:TPU:0, one launch (start us, length us, event | category | flops | bytes accessed | tf_op | source)
XLA Modules:
  0.0 111.4 jit_solution(4444039082128814350)
XLA Ops:
  0.6 0.0 copy-start
  0.6 1.2 %copy.18 = bf16[1,8,32,512]{3,1,2,0:T(8,128)(2,1)S(1)} copy(bf16[1,8,32,512]{3,2,1,0:T(8,128)(2,1)} %param.8) | data formatting | bytes 524288
  1.8 0.0 copy-start.4
  1.8 0.6 copy-done.4
  2.5 0.3 convolution_convert_fusion.6
  2.7 1.0 copy.19
  3.7 0.0 copy-start.5
  3.7 8.5 %all-to-all-start = ((bf16[16,32,512]{2,1,0:T(8,128)(2,1)}), bf16[16,32,512]{2,1,0:T(8,128)(2,1)S(1)}, u32[]{:S(2)}, u32[]{:S(2)}) async-start(bf16[16,32,512]{2,1,0:T(8,128)(2,1)} %bitcast.21), calls=%async_computation | async-start | bytes 1048576 | tf_op jit(solution)/shard_map/all_to_all | solution.py:54
  12.2 0.6 compare_reduce_fusion
  12.8 14.4 %all-to-all-done = bf16[16,32,512]{2,1,0:T(8,128)(2,1)S(1)} async-done(((bf16[16,32,512]{2,1,0:T(8,128)(2,1)}), bf16[16,32,512]{2,1,0:T(8,128)(2,1)S(1)}, u32[]{:S(2)}, u32[]{:S(2)}) %all-to-all-start) | async-done | bytes 524320 | tf_op jit(solution)/shard_map/all_to_all | solution.py:54
  27.3 0.0 copy-done
  27.3 0.0 copy-done.5
  27.3 1.5 %multiply_reduce_fusion.2 = (f32[]{:T(128)}, bf16[512,512]{1,0:T(8,128)(2,1)S(1)}) fusion(bf16[1,1,512,512]{3,2,1,0:T(8,128)(2,1)S(1)} %copy-done, bf16[512,512]{1,0:T(8,128)(2,1)S(1)} %bitcast.76, bf16[1,1,512,512]{3,2,1,0:T(8,128)(2,1)S(1)} %copy-done.5), kind=kOutput, calls=%fused_computation.53 | convolution fusion | flops 538181632 | bytes 2097156 | tf_op jit(solution)/shard_map/dot_general | solution.py:66
  28.8 0.9 copy.16
  29.7 0.5 broadcast.160
  30.2 3.8 %reduce.3 = bf16[512,512]{1,0:T(8,128)(2,1)S(1)} reduce(bf16[512,1,512]{2,1,0:T(2,128)(2,1)S(1)} %bitcast.78, bf16[]{:T(256)} %broadcast.160), dimensions={1}, to_apply=%bitcast.56.reduce_sub_computation | reduce | bytes 1048578
  34.0 1.2 %reshape.49 = bf16[16,2,8192]{2,1,0:T(2,128)(2,1)} reshape(bf16[512,512]{1,0:T(8,128)(2,1)S(1)} %reduce.3) | data formatting | bytes 1048576
  35.2 4.2 %all-to-all-start.1 = ((bf16[16,2,8192]{2,1,0:T(2,128)(2,1)}), bf16[16,2,8192]{2,1,0:T(2,128)(2,1)}, u32[]{:S(2)}, u32[]{:S(2)}) async-start(bf16[16,2,8192]{2,1,0:T(2,128)(2,1)} %reshape.49), calls=%async_computation.1 | async-start | bytes 1048576 | tf_op jit(solution)/shard_map/all_to_all | solution.py:76
  39.5 0.9 multiply_reduce_fusion.3
  40.3 1.4 %pad_maximum_fusion = f32[2]{0:T(128)S(1)} fusion(f32[1]{0:T(128)} %bitcast.6, f32[1]{0:T(128)} %bitcast.1), kind=kLoop, calls=%fused_computation.63 | loop fusion | flops 2 | bytes 16 | tf_op jit(solution)/shard_map/stack | solution.py:69
  41.7 0.1 broadcast_multiply_fusion
  42.4 40.7 %psum.7 = f32[2,8]{1,0:T(2,128)S(1)} all-reduce(f32[2,8]{1,0:T(2,128)S(1)} %broadcast_multiply_fusion), channel_id=1, replica_groups=mesh['dp'=16,'mp'=2] {'dp','mp'}, use_global_device_ids=true, to_apply=%region_2.0 | all-reduce | flops 16 | bytes 128 | tf_op jit(solution)/shard_map/psum | solution.py:77
  83.1 0.5 fusion.37
  83.6 0.0 copy-start.1
  83.6 1.5 %convolution_bitcast_fusion = f32[512,512]{1,0:T(8,128)} fusion(bf16[16,32,512]{2,1,0:T(8,128)(2,1)S(1)} %all-to-all-done), kind=kOutput, calls=%fused_computation.50 | convolution fusion | flops 268435456 | bytes 1572864 | tf_op jit(solution)/shard_map/ki,kj->ij/dot_general | solution.py:60
  85.1 0.0 copy-done.1
  85.1 18.9 %conditional.1 = (bf16[1,1,512,512]{3,2,1,0:T(8,128)(2,1)S(1)}, bf16[1,1,512,512]{3,2,1,0:T(8,128)(2,1)}) conditional(s32[]{:T(128)} %convert_element_type.101, () %tuple.22, (f32[1,1,512,512]{3,2,1,0:T(8,128)S(1)}, f32[512,512]{1,0:T(8,128)S(1)}, f32[1,1,512,512]{3,2,1,0:T(8,128)}, f32[512,512]{1,0:T(8,128)}) %tuple.39), branch_computations={%region_4.0_spmd, %region_5.0_spmd.clone} | conditional | flops 2166620160 | bytes 20971660 | solution.py:91
  85.1 0.9 multiply_reduce_fusion.1
  86.7 2.4 %multiply_reduce_fusion = f32[]{:T(128)} fusion(f32[512,512]{1,0:T(8,128)} %get-tuple-element.58, f32[1,1,512,512]{3,2,1,0:T(8,128)} %get-tuple-element.60), kind=kLoop, calls=%fused_computation.25 | loop fusion | flops 2097151 | bytes 2097156 | tf_op jit(solution)/shard_map/cond/branch_1_fun/reduce_sum | solution.py:18
  89.8 2.9 %fusion.7 = (bf16[512,512]{1,0:T(8,128)(2,1)S(1)}, bf16[512,512]{1,0:T(8,128)(2,1)}) fusion(f32[]{:T(128)S(6)} %sqrt.20, f32[512,512]{1,0:T(8,128)S(1)} %get-tuple-element.57, f32[1,1,512,512]{3,2,1,0:T(8,128)S(1)} %get-tuple-element.59, f32[]{:T(128)S(6)} %sqrt.21, f32[512,512]{1,0:T(8,128)} %get-tuple-element.58, f32[1,1,512,512]{3,2,1,0:T(8,128)} %get-tuple-element.60), kind=kLoop, calls=%fused_computation.19 | loop fusion | flops 4980736 | bytes 5242888 | tf_op jit(solution)/shard_map/cond/branch_1_fun/convert_element_type | solution.py:22
  92.7 0.0 copy-start.3
  92.7 3.6 %convolution_convert_fusion.1 = bf16[512,512]{1,0:T(8,128)(2,1)} fusion(bf16[512,512]{1,0:T(8,128)(2,1)} %get-tuple-element.75), kind=kOutput, calls=%fused_computation.9 | convolution fusion | flops 537395200 | bytes 1048576 | tf_op jit(solution)/shard_map/cond/branch_1_fun/dot_general | solution.py:33
  96.4 3.5 %fusion.5 = bf16[1,1,512,512]{3,2,1,0:T(8,128)(2,1)} fusion(bf16[512,512]{1,0:T(8,128)(2,1)} %convolution_convert_fusion.1, bf16[512,512]{1,0:T(8,128)(2,1)} %get-tuple-element.75, f32[]{:T(128)S(6)} %pow.9, f32[]{:T(128)S(6)} %sqrt.21, f32[1,1,512,512]{3,2,1,0:T(8,128)} %get-tuple-element.60, f32[512,512]{1,0:T(8,128)} %get-tuple-element.58), kind=kOutput, calls=%fused_computation.17 | convolution fusion | flops 541327360 | bytes 3670024 | tf_op jit(solution)/shard_map/cond/branch_1_fun/dot_general | solution.py:26
  99.9 0.0 copy-done.3
  99.9 1.8 %convolution_convert_fusion.4 = bf16[512,512]{1,0:T(8,128)(2,1)} fusion(bf16[512,512]{1,0:T(8,128)(2,1)S(1)} %get-tuple-element.74), kind=kOutput, calls=%fused_computation.12 | convolution fusion | flops 537395200 | bytes 1048576 | tf_op jit(solution)/shard_map/cond/branch_1_fun/dot_general | solution.py:33
  101.8 2.1 %fusion.4 = bf16[1,1,512,512]{3,2,1,0:T(8,128)(2,1)S(1)} fusion(bf16[512,512]{1,0:T(8,128)(2,1)} %convolution_convert_fusion.4, bf16[512,512]{1,0:T(8,128)(2,1)} %copy-done.3, f32[]{:T(128)S(6)} %pow.8, f32[]{:T(128)S(6)} %sqrt.20, f32[1,1,512,512]{3,2,1,0:T(8,128)S(1)} %get-tuple-element.59, f32[512,512]{1,0:T(8,128)S(1)} %get-tuple-element.57), kind=kOutput, calls=%fused_computation.16 | convolution fusion | flops 541327360 | bytes 3670024 | tf_op jit(solution)/shard_map/cond/branch_1_fun/dot_general | solution.py:26
  104.0 0.0 copy-start.2
  104.0 0.8 copy-done.2
  104.8 0.0 all-to-all-done.1
  104.8 2.2 %reshape.50 = bf16[512,1,512]{2,1,0:T(2,128)(2,1)S(1)} reshape(bf16[16,2,8192]{2,1,0:T(2,128)(2,1)} %all-to-all-done.1) | data formatting | bytes 1048576
  107.0 3.1 %bitcast_reduce_fusion = bf16[512,512]{1,0:T(8,128)(2,1)S(1)} fusion(bf16[512,1,512]{2,1,0:T(2,128)(2,1)S(1)} %reshape.50), kind=kLoop, calls=%fused_computation.67 | loop fusion | bytes 1048576 | tf_op jit(solution)/shard_map/all_to_all | solution.py:76
  110.1 0.2 reshape.40
  110.4 0.3 fusion.28
  110.7 0.8 copy.17
  (2 shorter events, 0.0 us)
Async XLA Ops:
  0.6 26.6 %copy-start = (bf16[1,1,512,512]{3,2,1,0:T(8,128)(2,1)S(1)}, bf16[1,1,512,512]{3,2,1,0:T(8,128)(2,1)}, u32[]{:S(2)}) copy-start(bf16[1,1,512,512]{3,2,1,0:T(8,128)(2,1)} %param.12) | copy-start | bytes 1572868
  1.8 0.7 copy-start.4
  3.7 23.6 %copy-start.5 = (bf16[1,1,512,512]{3,2,1,0:T(8,128)(2,1)S(1)}, bf16[1,1,512,512]{3,2,1,0:T(8,128)(2,1)}, u32[]{:S(2)}) copy-start(bf16[1,1,512,512]{3,2,1,0:T(8,128)(2,1)} %param.13) | copy-start | bytes 1572868
  3.7 23.6 %all-to-all-start = ((bf16[16,32,512]{2,1,0:T(8,128)(2,1)}), bf16[16,32,512]{2,1,0:T(8,128)(2,1)S(1)}, u32[]{:S(2)}, u32[]{:S(2)}) async-start(bf16[16,32,512]{2,1,0:T(8,128)(2,1)} %bitcast.21), calls=%async_computation | async-start | bytes 1048576 | tf_op jit(solution)/shard_map/all_to_all | solution.py:54
  35.2 69.6 %all-to-all-start.1 = ((bf16[16,2,8192]{2,1,0:T(2,128)(2,1)}), bf16[16,2,8192]{2,1,0:T(2,128)(2,1)}, u32[]{:S(2)}, u32[]{:S(2)}) async-start(bf16[16,2,8192]{2,1,0:T(2,128)(2,1)} %reshape.49), calls=%async_computation.1 | async-start | bytes 1048576 | tf_op jit(solution)/shard_map/all_to_all | solution.py:76
  83.6 1.5 %copy-start.1 = (f32[1,1,512,512]{3,2,1,0:T(8,128)S(1)}, f32[1,1,512,512]{3,2,1,0:T(8,128)}, u32[]{:S(2)}) copy-start(f32[1,1,512,512]{3,2,1,0:T(8,128)} %param.10) | copy-start | bytes 3145732
  92.7 7.2 %copy-start.3 = (bf16[512,512]{1,0:T(8,128)(2,1)}, bf16[512,512]{1,0:T(8,128)(2,1)S(1)}, u32[]{:S(2)}) copy-start(bf16[512,512]{1,0:T(8,128)(2,1)S(1)} %get-tuple-element.74) | copy-start | bytes 1572868 | tf_op jit(solution)/shard_map/cond
  104.0 0.8 copy-start.2
where the time goes:
time: 112 us; the launch traced here: 111 us
  blocking collectives  40.7 us (36%)
  matrix products  15 us (13%)
  waiting for transfers between devices  14.4 us (13%)
  other arithmetic  13 us (12%)
  starting transfers between devices  12.7 us (11%)
  local copies, waits for them, and re-layouts  12.5 us (11%)
  loops' own time  1.68 us (2%)
  between operations  1.41 us (1%)
    psum x1, blocking collectives, shards(): totals = lax.psum(graft_terms, ('dp', 'mp'))  40.7 us
    all_to_all x1, waiting for transfers between devices, shards(): lax.all_to_all(outgoing, 'dp', split_axis=0, concat_axis=1, tiled=True)  14.4 us
    all_to_all x1, starting transfers between devices, shards(): lax.all_to_all(outgoing, 'dp', split_axis=0, concat_axis=1, tiled=True)  8.47 us
    unnamed x16, local copies, waits for them, and re-layouts  8.25 us
    dot_general x2, matrix products, newton_root(): jnp.dot(iterate.astype(jnp.bfloat16), factor, preferred_element_type=jnp....  5.58 us
    dot_general x2, matrix products, newton_root(): jnp.dot(factor_two, factor_two, preferred_element_type=jnp.float32)  5.42 us
    all_to_all x1, starting transfers between devices, shards(): lax.all_to_all(direction[None], 'dp', split_axis=1, concat_axis=0, tiled=...  4.23 us
    unnamed x1, other arithmetic  3.82 us
  transfers between devices with their start and end apart: 2, of which 1 were waited for; matrix products, arithmetic and copies ran while one was open for 20% of the time, Pallas kernels for 0%

commit v1 on v0

v1 whole, which is shorter than its diff:
```python
import functools

import jax
import jax.numpy as jnp
from jax import lax
from jax.experimental import pallas as pl
from jax.experimental.pallas import tpu as pltpu
from jax.sharding import PartitionSpec as P

ITERS = 2

stat_decay = 0.9
ridge_term = 0.001
tiny_term = 1e-06

MESH = pl.DeviceIdType.MESH


def mm(a, b, dims=((1,), (0,))):
    return lax.dot_general(a, b, (dims, ((), ())), preferred_element_type=jnp.float32)


def eye(n):
    rows = lax.broadcasted_iota(jnp.int32, (n, n), 0)
    cols = lax.broadcasted_iota(jnp.int32, (n, n), 1)
    return rows == cols


def newton_root(shifted):
    diag = eye(shifted.shape[0])
    scale = jnp.sqrt(jnp.sum(shifted * shifted, keepdims=True) + tiny_term)
    matrix = shifted / scale
    iterate = None
    for k in range(ITERS):
        factor = ((jnp.where(diag, 5.0, 0.0) - matrix) / 4.0).astype(jnp.bfloat16)
        if k == 0:
            iterate = jnp.exp(-0.25 * jnp.log(scale)) * factor.astype(jnp.float32)
        else:
            iterate = mm(iterate.astype(jnp.bfloat16), factor)
        if k + 1 < ITERS:
            two = mm(factor, factor).astype(jnp.bfloat16)
            four = mm(two, two).astype(jnp.bfloat16)
            matrix = mm(four, matrix.astype(jnp.bfloat16))
    return iterate


def kernel(
    n_dp, n_mp,
    owners, grad_hbm, lstat_hbm, rstat_hbm, lroot_hbm, rroot_hbm,
    update_hbm, lout_hbm, rout_hbm,
    grad, lstat, rstat, lroot, rroot,
    outgoing, arrived, direction, returned, upd, lout, rout,
    norm_out, norm_in, row_out, row_in,
    load_sem, store_sem, gs_sem, gr_sem, ds_sem, dr_sem, ns_sem, nr_sem, rs_sem, rr_sem,
):
    me = lax.axis_index("dp")
    mine = lax.axis_index("mp")
    nb, rows, width = grad.shape
    half = n_dp // 2

    loads = [
        pltpu.make_async_copy(src, dst, load_sem.at[i])
        for i, (src, dst) in enumerate(
            [(grad_hbm, grad), (rroot_hbm, rroot), (lroot_hbm, lroot), (lstat_hbm, lstat), (rstat_hbm, rstat)]
        )
    ]
    for load in loads:
        load.start()

    barrier = pltpu.get_barrier_semaphore()

    def greet_dp(i, carry):
        pl.semaphore_signal(barrier, inc=1, device_id=(lax.rem(me + i, n_dp), mine), device_id_type=MESH)
        return carry

    def greet_mp(i, carry):
        pl.semaphore_signal(barrier, inc=1, device_id=(me, lax.rem(mine + i, n_mp)), device_id_type=MESH)
        return carry

    lax.fori_loop(1, n_dp, greet_dp, 0)
    lax.fori_loop(1, n_mp, greet_mp, 0)

    busy = lax.fori_loop(0, nb, lambda j, a: a + (owners[0, j] == me).astype(jnp.int32), 0)
    busy_f = busy.astype(jnp.float32)

    loads[0].wait()

    def arrange(c, carry):
        j = lax.fori_loop(
            0, nb, lambda b, a: jnp.where(lax.rem(owners[0, b], half) == c, b, a), 0
        )
        outgoing[c] = grad[j]
        return carry

    lax.fori_loop(0, half, arrange, 0)

    pl.semaphore_wait(barrier, n_dp - 1 + n_mp - 1)

    def send_grad(i):
        peer = lax.rem(me + i, n_dp)
        return pltpu.make_async_remote_copy(
            src_ref=outgoing.at[lax.rem(peer, half)], dst_ref=arrived.at[me],
            send_sem=gs_sem.at[peer], recv_sem=gr_sem.at[me],
            device_id=(peer, mine), device_id_type=MESH,
        )

    def take_grad(i):
        peer = lax.rem(me + i, n_dp)
        return pltpu.make_async_remote_copy(
            src_ref=outgoing.at[lax.rem(peer, half)], dst_ref=arrived.at[peer],
            send_sem=gs_sem.at[peer], recv_sem=gr_sem.at[peer],
            device_id=(peer, mine), device_id_type=MESH,
        )

    def send_dir(i):
        peer = lax.rem(me + i, n_dp)
        return pltpu.make_async_remote_copy(
            src_ref=direction.at[peer], dst_ref=returned.at[me],
            send_sem=ds_sem.at[peer], recv_sem=dr_sem.at[me],
            device_id=(peer, mine), device_id_type=MESH,
        )

    def take_dir(i):
        peer = lax.rem(me + i, n_dp)
        return pltpu.make_async_remote_copy(
            src_ref=direction.at[peer], dst_ref=returned.at[peer],
            send_sem=ds_sem.at[peer], recv_sem=dr_sem.at[peer],
            device_id=(peer, mine), device_id_type=MESH,
        )

    def send_norm(i):
        peer = lax.rem(me + i, n_dp)
        return pltpu.make_async_remote_copy(
            src_ref=norm_out, dst_ref=norm_in.at[me],
            send_sem=ns_sem.at[peer], recv_sem=nr_sem.at[me],
            device_id=(peer, mine), device_id_type=MESH,
        )

    def take_norm(i):
        peer = lax.rem(me + i, n_dp)
        return pltpu.make_async_remote_copy(
            src_ref=norm_out, dst_ref=norm_in.at[peer],
            send_sem=ns_sem.at[peer], recv_sem=nr_sem.at[peer],
            device_id=(peer, mine), device_id_type=MESH,
        )

    def send_row(i):
        peer = lax.rem(mine + i, n_mp)
        return pltpu.make_async_remote_copy(
            src_ref=row_out, dst_ref=row_in.at[mine],
            send_sem=rs_sem.at[peer], recv_sem=rr_sem.at[mine],
            device_id=(me, peer), device_id_type=MESH,
        )

    def take_row(i):
        peer = lax.rem(mine + i, n_mp)
        return pltpu.make_async_remote_copy(
            src_ref=row_out, dst_ref=row_in.at[peer],
            send_sem=rs_sem.at[peer], recv_sem=rr_sem.at[peer],
            device_id=(me, peer), device_id_type=MESH,
        )

    def each(count, action):
        def step(i, carry):
            action(i)
            return carry

        lax.fori_loop(1, count, step, 0)

    def joined(ref):
        if rows % 16 == 0:
            return ref[...].reshape(n_dp * rows, width)
        return ref[...].astype(jnp.float32).reshape(n_dp * rows, width).astype(jnp.bfloat16)

    def split(value):
        if rows % 16 == 0:
            return value.reshape(n_dp, rows, width)
        return value.astype(jnp.float32).reshape(n_dp, rows, width).astype(jnp.bfloat16)

    each(n_dp, lambda i: send_grad(i).start())
    arrived[me] = outgoing[lax.rem(me, half)]
    loads[1].wait()
    loads[2].wait()
    each(n_dp, lambda i: take_grad(i).wait_recv())

    block = joined(arrived)
    shaded = mm(block, rroot[...]).astype(jnp.bfloat16)
    moved = mm(lroot[...], shaded).astype(jnp.bfloat16)
    direction[...] = split(moved)
    each(n_dp, lambda i: send_dir(i).start())
    returned[me] = direction[me]

    block32 = block.astype(jnp.float32)
    moved32 = moved.astype(jnp.float32)
    g_sum = jnp.sum(block32 * block32, keepdims=True) * busy_f
    d_sum = jnp.sum(moved32 * moved32, keepdims=True) * busy_f
    sub = lax.broadcasted_iota(jnp.int32, (8, 128), 0)
    lane = lax.broadcasted_iota(jnp.int32, (8, 128), 1)
    norm_out[...] = jnp.where(sub < 4, g_sum, d_sum)
    each(n_dp, lambda i: send_norm(i).start())
    norm_in[me] = norm_out[...]

    diag = eye(width)

    def refresh(stat, gram, out):
        shifted = (stat_decay * stat[...] + gram / width) + jnp.where(diag, ridge_term, 0.0)
        root = newton_root(shifted)
        out[...] = jnp.where(busy > 0, root, 0.0).astype(jnp.bfloat16)

    loads[3].wait()
    refresh(lstat, mm(block, block, ((1,), (1,))), lout)
    lcopy = pltpu.make_async_copy(lout, lout_hbm, store_sem.at[0])
    lcopy.start()

    each(n_dp, lambda i: take_norm(i).wait_recv())
    row_out[...] = lax.fori_loop(
        0, nb, lambda j, a: jnp.where(lane == j, norm_in[owners[0, j]], a), jnp.zeros((8, 128), jnp.float32)
    )
    each(n_mp, lambda i: send_row(i).start())
    row_in[mine] = row_out[...]

    loads[4].wait()
    refresh(rstat, mm(block, block, ((0,), (0,))), rout)
    rcopy = pltpu.make_async_copy(rout, rout_hbm, store_sem.at[1])
    rcopy.start()

    each(n_mp, lambda i: take_row(i).wait_recv())
    totals = lax.fori_loop(0, n_mp, lambda i, a: a + row_in[i], jnp.zeros((8, 128), jnp.float32))
    graft = jnp.sqrt(totals[0:1] / (totals[4:5] + tiny_term))
    lane1 = lax.broadcasted_iota(jnp.int32, (1, 128), 1)

    each(n_dp, lambda i: take_dir(i).wait_recv())

    def finish(j, carry):
        factor = jnp.sum(jnp.where(lane1 == j, graft, 0.0), keepdims=True)
        upd[j] = (factor * returned[owners[0, j]].astype(jnp.float32)).astype(jnp.bfloat16)
        return carry

    lax.fori_loop(0, nb, finish, 0)
    ucopy = pltpu.make_async_copy(upd, update_hbm, store_sem.at[2])
    ucopy.start()

    each(n_dp, lambda i: send_grad(i).wait_send())
    each(n_dp, lambda i: send_dir(i).wait_send())
    each(n_dp, lambda i: send_norm(i).wait_send())
    each(n_mp, lambda i: send_row(i).wait_send())
    lcopy.wait()
    rcopy.wait()
    ucopy.wait()


def shards(n_dp, n_mp, gradient, owners, left_stats, right_stats, left_roots_old, right_roots_old):
    _, nb, rows, width = gradient.shape
    half = n_dp // 2
    any_spec = pl.BlockSpec(memory_space=pl.ANY)
    bf16, f32 = jnp.bfloat16, jnp.float32
    dma = pltpu.SemaphoreType.DMA
    square = jax.ShapeDtypeStruct((width, width), bf16)
    update, left, right = pl.pallas_call(
        functools.partial(kernel, n_dp, n_mp),
        out_shape=(jax.ShapeDtypeStruct((nb, rows, width), bf16), square, square),
        in_specs=[pl.BlockSpec(memory_space=pltpu.SMEM)] + [any_spec] * 5,
        out_specs=(any_spec,) * 3,
        scratch_shapes=[
            pltpu.VMEM((nb, rows, width), bf16),
            pltpu.VMEM((width, width), f32),
            pltpu.VMEM((width, width), f32),
            pltpu.VMEM((width, width), bf16),
            pltpu.VMEM((width, width), bf16),
            pltpu.VMEM((half, rows, width), bf16),
            pltpu.VMEM((n_dp, rows, width), bf16),
            pltpu.VMEM((n_dp, rows, width), bf16),
            pltpu.VMEM((n_dp, rows, width), bf16),
            pltpu.VMEM((nb, rows, width), bf16),
            pltpu.VMEM((width, width), bf16),
            pltpu.VMEM((width, width), bf16),
            pltpu.VMEM((8, 128), f32),
            pltpu.VMEM((n_dp, 8, 128), f32),
            pltpu.VMEM((8, 128), f32),
            pltpu.VMEM((n_mp, 8, 128), f32),
            dma((5,)), dma((3,)),
            dma((n_dp,)), dma((n_dp,)), dma((n_dp,)), dma((n_dp,)), dma((n_dp,)), dma((n_dp,)),
            dma((n_mp,)), dma((n_mp,)),
        ],
        compiler_params=pltpu.CompilerParams(
            collective_id=0, has_side_effects=True
        ),
    )(owners, gradient[0], left_stats[0, 0], right_stats[0, 0], left_roots_old[0, 0], right_roots_old[0, 0])
    return update[None], left[None, None], right[None, None]


def solution(mesh):
    return jax.shard_map(
        functools.partial(shards, mesh.shape["dp"], mesh.shape["mp"]),
        mesh=mesh,
        in_specs=(
            P("mp", None, "dp", None),
            P("mp", None),
            P("mp", "dp", None, None),
            P("mp", "dp", None, None),
            P("mp", "dp", None, None),
            P("mp", "dp", None, None),
        ),
        out_specs=(P("mp", None, "dp", None), P("mp", "dp", None, None), P("mp", "dp", None, None)),
        check_vma=False,
    )
```

time: 112 us -> 44.3 us (0.40)
  the two profiles are of different devices: /device:TPU:0 before, /device:TPU:25 now
where the time goes in v1:
time: 44.3 us; the launch traced here: 43.9 us
  Pallas kernels  39.5 us (89%)
  local copies, waits for them, and re-layouts  3.75 us (8%)
  between operations  0.65 us (1%)
    pallas_call x1, Pallas kernels, shards(): pl.pallas_call(functools.partial(kernel, n_dp, n_mp), out_shape=(jax.Shap...  39.5 us
    unnamed x7, local copies, waits for them, and re-layouts  3.75 us

profile of v1, /device:TPU:25, one launch (start us, length us, event | category | flops | bytes accessed | tf_op | source)
XLA Modules:
  0.0 43.9 jit_solution(6006269477762492320)
XLA Ops:
  0.6 39.5 %shard_map.85 = (bf16[8,32,512]{2,1,0:T(8,128)(2,1)}, bf16[512,512]{1,0:T(8,128)(2,1)}, bf16[512,512]{1,0:T(8,128)(2,1)}) custom-call(s32[1,8]{1,0:T(1,128)} %owners.1, bf16[8,32,512]{2,1,0:T(8,128)(2,1)} %bitcast.14, f32[512,512]{1,0:T(8,128)} %bitcast.8, f32[512,512]{1,0:T(8,128)} %bitcast.9, bf16[512,512]{1,0:T(8,128)(2,1)} %bitcast.12, ...), custom_call_target="tpu_custom_call" | custom-call | tf_op jit(solution)/shard_map/pallas_call | solution.py:259
  40.2 0.0 copy-start.1
  40.2 1.7 %copy.12 = bf16[1,8,32,512]{3,2,1,0:T(8,128)(2,1)} copy(bf16[1,8,32,512]{3,2,1,0:T(8,128)(2,1)} %bitcast.15) | data formatting | bytes 524288
  41.9 0.0 copy-done.1
  41.9 0.0 copy-start
  41.9 0.8 %copy.13 = bf16[1,1,512,512]{3,2,1,0:T(8,128)(2,1)} copy(bf16[1,1,512,512]{3,2,1,0:T(8,128)(2,1)S(1)} %bitcast.11) | data formatting | bytes 1048576
  42.7 0.4 copy-done
  43.1 0.8 %copy.14 = bf16[1,1,512,512]{3,2,1,0:T(8,128)(2,1)} copy(bf16[1,1,512,512]{3,2,1,0:T(8,128)(2,1)S(1)} %bitcast.10) | data formatting | bytes 1048576
Async XLA Ops:
  40.2 1.7 %copy-start.1 = (bf16[512,512]{1,0:T(8,128)(2,1)S(1)}, bf16[512,512]{1,0:T(8,128)(2,1)}, u32[]{:S(2)}) copy-start(bf16[512,512]{1,0:T(8,128)(2,1)} %get-tuple-element.7) | copy-start | bytes 1572868
  41.9 1.2 %copy-start = (bf16[512,512]{1,0:T(8,128)(2,1)S(1)}, bf16[512,512]{1,0:T(8,128)(2,1)}, u32[]{:S(2)}) copy-start(bf16[512,512]{1,0:T(8,128)(2,1)} %get-tuple-element.8) | copy-start | bytes 1572868

commit v2 on v1

v2 whole, which is shorter than its diff:
```python
import functools

import jax
import jax.numpy as jnp
from jax import lax
from jax.experimental import pallas as pl
from jax.experimental.pallas import tpu as pltpu
from jax.sharding import PartitionSpec as P

ITERS = 2

stat_decay = 0.9
ridge_term = 0.001
tiny_term = 1e-06

MESH = pl.DeviceIdType.MESH


def mm(a, b, dims=((1,), (0,))):
    return lax.dot_general(a, b, (dims, ((), ())), preferred_element_type=jnp.float32)


def eye(n):
    rows = lax.broadcasted_iota(jnp.int32, (n, n), 0)
    cols = lax.broadcasted_iota(jnp.int32, (n, n), 1)
    return rows == cols


def newton_root(shifted):
    diag = eye(shifted.shape[0])
    scale = jnp.sqrt(jnp.sum(shifted * shifted, keepdims=True) + tiny_term)
    matrix = shifted / scale
    iterate = None
    for k in range(ITERS):
        factor = ((jnp.where(diag, 5.0, 0.0) - matrix) / 4.0).astype(jnp.bfloat16)
        if k == 0:
            iterate = jnp.exp(-0.25 * jnp.log(scale)) * factor.astype(jnp.float32)
        else:
            iterate = mm(iterate.astype(jnp.bfloat16), factor)
        if k + 1 < ITERS:
            two = mm(factor, factor).astype(jnp.bfloat16)
            four = mm(two, two).astype(jnp.bfloat16)
            matrix = mm(four, matrix.astype(jnp.bfloat16))
    return iterate


def kernel(
    n_dp, n_mp,
    owners, grad_hbm, lstat_hbm, rstat_hbm, lroot_hbm, rroot_hbm,
    upd, lout, rout,
    grad, lstat, rstat, roots,
    stay, go, outgoing, arrived, direction, returned,
    norm_out, norm_in, row_out, row_in,
    load_sem, swap_sem, gs_sem, gr_sem, gf_sem, ds_sem, dr_sem, df_sem,
    ns_sem, nr_sem, rs_sem, rr_sem,
):
    me = lax.axis_index("dp")
    mine = lax.axis_index("mp")
    nb, rows, width = grad.shape
    half = n_dp // 2
    quarter = half // 2
    side = mine // (n_mp // 2)
    partner = lax.rem(mine + n_mp // 2, n_mp)
    kept = lax.rem(side + me, 2)
    given = 1 - kept

    loads = [
        pltpu.make_async_copy(src, dst, load_sem.at[i])
        for i, (src, dst) in enumerate(
            [
                (grad_hbm, grad),
                (rroot_hbm, roots.at[0, 1]),
                (lroot_hbm, roots.at[0, 0]),
                (lstat_hbm, lstat),
                (rstat_hbm, rstat),
            ]
        )
    ]
    for load in loads:
        load.start()

    def each(first, last, action):
        def step(i, carry):
            action(i)
            return carry

        lax.fori_loop(first, last, step, 0)

    barrier = pltpu.get_barrier_semaphore()

    def greet(dp, mp):
        pl.semaphore_signal(barrier, inc=1, device_id=(dp, mp), device_id_type=MESH)

    each(1, n_dp, lambda i: greet(lax.rem(me + i, n_dp), mine))
    each(1, n_mp, lambda i: greet(me, lax.rem(mine + i, n_mp)))

    def holds(owner):
        return lax.fori_loop(0, nb, lambda j, a: jnp.where(owners[0, j] == owner, 1, a), 0)

    def block_of(corner):
        return lax.fori_loop(
            0, nb, lambda j, a: jnp.where(lax.rem(owners[0, j], half) == corner, j, a), 0
        )

    busy = holds(me)

    loads[0].wait()

    def arrange(i):
        go[i] = grad[block_of(2 * i + given)]
        stay[0, i] = grad[block_of(2 * i + kept)]

    each(0, quarter, arrange)

    def remote(src, dst, send, recv, dp, mp):
        return pltpu.make_async_remote_copy(
            src_ref=src, dst_ref=dst, send_sem=send, recv_sem=recv,
            device_id=(dp, mp), device_id_type=MESH,
        )

    pl.semaphore_wait(barrier, n_dp - 1 + n_mp - 1)

    swap = remote(go, stay.at[1], swap_sem.at[0], swap_sem.at[1], me, partner)
    swap.start()
    loads[1].wait()
    swap_r = remote(roots.at[0, 1], roots.at[1, 1], swap_sem.at[2], swap_sem.at[3], me, partner)
    loads[2].wait()
    swap_l = remote(roots.at[0, 0], roots.at[1, 0], swap_sem.at[4], swap_sem.at[5], me, partner)

    first = 1 - side

    def ahead(d):
        return lax.rem(me + side + 2 * d, n_dp)

    def behind(d):
        return lax.rem(me + 2 * n_dp - side - 2 * d, n_dp)

    def across(d):
        return lax.rem(me + 2 * n_dp - (1 - side) - 2 * d, n_dp)

    def grad_out(peer):
        return remote(outgoing.at[peer // 2], arrived.at[me], gs_sem.at[peer], gr_sem.at[me], peer, mine)

    def grad_in(peer):
        return remote(outgoing.at[peer // 2], arrived.at[peer], gs_sem.at[peer], gr_sem.at[peer], peer, mine)

    def grad_on(peer):
        return remote(arrived.at[peer], arrived.at[peer], gf_sem.at[peer], gr_sem.at[peer], me, partner)

    def dir_out(peer):
        return remote(direction.at[peer], returned.at[me], ds_sem.at[peer], dr_sem.at[me], peer, mine)

    def dir_in(peer):
        return remote(direction.at[peer], returned.at[peer], ds_sem.at[peer], dr_sem.at[peer], peer, mine)

    def dir_on(peer):
        return remote(returned.at[peer], returned.at[peer], df_sem.at[peer], dr_sem.at[peer], me, partner)

    def norm_to(peer):
        return remote(norm_out, norm_in.at[me], ns_sem.at[peer], nr_sem.at[me], peer, mine)

    def norm_from(peer):
        return remote(norm_out, norm_in.at[peer], ns_sem.at[peer], nr_sem.at[peer], peer, mine)

    def row_to(peer):
        return remote(row_out, row_in.at[mine], rs_sem.at[peer], rr_sem.at[mine], me, peer)

    def row_from(peer):
        return remote(row_out, row_in.at[peer], rs_sem.at[peer], rr_sem.at[peer], me, peer)

    def joined(value):
        if rows % 16 == 0:
            return value.reshape(n_dp * rows, width)
        return value.astype(jnp.float32).reshape(n_dp * rows, width).astype(jnp.bfloat16)

    def split(value):
        if rows % 16 == 0:
            return value.reshape(n_dp, rows, width)
        return value.astype(jnp.float32).reshape(n_dp, rows, width).astype(jnp.bfloat16)

    swap.wait_recv()

    def dispatch(d):
        peer = ahead(d)
        outgoing[peer // 2] = stay[1 - holds(peer), lax.rem(peer // 2, quarter)]
        grad_out(peer).start()

    each(first, half, dispatch)
    swap_r.start()
    swap_l.start()

    @pl.when(side == 0)
    def _():
        arrived[me] = stay[1 - busy, lax.rem(me // 2, quarter)]
        grad_on(me).start()

    def pass_grad(d):
        grad_in(behind(d)).wait_recv()
        grad_on(behind(d)).start()

    each(first, half, pass_grad)
    swap_r.wait_recv()
    swap_l.wait_recv()
    each(0, half, lambda d: grad_on(across(d)).wait_recv())

    block = joined(arrived[...])
    shaded = mm(block, roots[1 - busy, 1]).astype(jnp.bfloat16)
    moved = mm(roots[1 - busy, 0], shaded).astype(jnp.bfloat16)
    direction[...] = split(moved)
    block32 = block.astype(jnp.float32)
    moved32 = moved.astype(jnp.float32)
    g_sum = jnp.sum(block32 * block32, keepdims=True)
    d_sum = jnp.sum(moved32 * moved32, keepdims=True)
    sub = lax.broadcasted_iota(jnp.int32, (2, 128), 0)
    lane = lax.broadcasted_iota(jnp.int32, (2, 128), 1)
    norm_out[...] = jnp.where(sub == 0, g_sum, d_sum)
    each(1, n_dp, lambda i: norm_to(lax.rem(me + i, n_dp)).start())
    each(first, half, lambda d: dir_out(ahead(d)).start())
    norm_in[me] = norm_out[...]
    returned[me] = direction[me]

    diag = eye(width)

    def refresh(stat, gram, out):
        shifted = (stat_decay * stat[...] + gram / width) + jnp.where(diag, ridge_term, 0.0)
        root = newton_root(shifted)
        out[...] = jnp.where(busy > 0, root, 0.0).astype(jnp.bfloat16)

    def pass_dir(d):
        dir_in(behind(d)).wait_recv()
        dir_on(behind(d)).start()

    loads[3].wait()
    refresh(lstat, mm(block, block, ((1,), (1,))), lout)

    each(1, n_dp, lambda i: norm_from(lax.rem(me + i, n_dp)).wait_recv())
    row_out[...] = lax.fori_loop(
        0, nb, lambda j, a: jnp.where(lane == j, norm_in[owners[0, j]], a), jnp.zeros((2, 128), jnp.float32)
    )
    each(1, n_mp, lambda i: row_to(lax.rem(mine + i, n_mp)).start())
    row_in[mine] = row_out[...]

    loads[4].wait()
    refresh(rstat, mm(block, block, ((0,), (0,))), rout)

    each(first, half, pass_dir)

    each(1, n_mp, lambda i: row_from(lax.rem(mine + i, n_mp)).wait_recv())
    totals = lax.fori_loop(0, n_mp, lambda i, a: a + row_in[i], jnp.zeros((2, 128), jnp.float32))
    graft = jnp.sqrt(totals[0:1] / (totals[1:2] + tiny_term))
    lane1 = lax.broadcasted_iota(jnp.int32, (1, 128), 1)

    each(1 - first, half, lambda d: dir_on(across(d)).wait_recv())

    def finish(j):
        factor = jnp.sum(jnp.where(lane1 == j, graft, 0.0), keepdims=True)
        upd[j] = (factor * returned[owners[0, j]].astype(jnp.float32)).astype(jnp.bfloat16)

    each(0, nb, finish)

    swap.wait_send()
    swap_r.wait_send()
    swap_l.wait_send()
    each(first, half, lambda d: grad_out(ahead(d)).wait_send())
    each(0, half, lambda d: grad_on(behind(d)).wait_send())
    each(first, half, lambda d: dir_out(ahead(d)).wait_send())
    each(first, half, lambda d: dir_on(behind(d)).wait_send())
    each(1, n_dp, lambda i: norm_to(lax.rem(me + i, n_dp)).wait_send())
    each(1, n_mp, lambda i: row_to(lax.rem(mine + i, n_mp)).wait_send())


def shards(n_dp, n_mp, gradient, owners, left_stats, right_stats, left_roots_old, right_roots_old):
    _, nb, rows, width = gradient.shape
    half = n_dp // 2
    hbm = pl.BlockSpec(memory_space=pltpu.HBM)
    vmem = pl.BlockSpec(memory_space=pltpu.VMEM)
    bf16, f32 = jnp.bfloat16, jnp.float32
    dma = pltpu.SemaphoreType.DMA
    square = jax.ShapeDtypeStruct((width, width), bf16)
    update, left, right = pl.pallas_call(
        functools.partial(kernel, n_dp, n_mp),
        out_shape=(jax.ShapeDtypeStruct((nb, rows, width), bf16), square, square),
        in_specs=[pl.BlockSpec(memory_space=pltpu.SMEM)] + [hbm] * 5,
        out_specs=(vmem,) * 3,
        scratch_shapes=[
            pltpu.VMEM((nb, rows, width), bf16),
            pltpu.VMEM((width, width), f32),
            pltpu.VMEM((width, width), f32),
            pltpu.VMEM((2, 2, width, width), bf16),
            pltpu.VMEM((2, half // 2, rows, width), bf16),
            pltpu.VMEM((half // 2, rows, width), bf16),
            pltpu.VMEM((half, rows, width), bf16),
            pltpu.VMEM((n_dp, rows, width), bf16),
            pltpu.VMEM((n_dp, rows, width), bf16),
            pltpu.VMEM((n_dp, rows, width), bf16),
            pltpu.VMEM((2, 128), f32),
            pltpu.VMEM((n_dp, 2, 128), f32),
            pltpu.VMEM((2, 128), f32),
            pltpu.VMEM((n_mp, 2, 128), f32),
            dma((5,)), dma((6,)),
            *[dma((n_dp,)) for _ in range(8)],
            dma((n_mp,)), dma((n_mp,)),
        ],
        compiler_params=pltpu.CompilerParams(
            collective_id=0, has_side_effects=True
        ),
    )(owners, gradient[0], left_stats[0, 0], right_stats[0, 0], left_roots_old[0, 0], right_roots_old[0, 0])
    return update[None], left[None, None], right[None, None]


def solution(mesh):
    return jax.shard_map(
        functools.partial(shards, mesh.shape["dp"], mesh.shape["mp"]),
        mesh=mesh,
        in_specs=(
            P("mp", None, "dp", None),
            P("mp", None),
            P("mp", "dp", None, None),
            P("mp", "dp", None, None),
            P("mp", "dp", None, None),
            P("mp", "dp", None, None),
        ),
        out_specs=(P("mp", None, "dp", None), P("mp", "dp", None, None), P("mp", "dp", None, None)),
        check_vma=False,
    )
```

time: 44.3 us -> 34.9 us (0.79)
  the two profiles are of different devices: /device:TPU:25 before, /device:TPU:1 now
where the time goes in v2:
time: 34.9 us; the launch traced here: 34.7 us
  Pallas kernels  30.3 us (87%)
  local copies, waits for them, and re-layouts  3.75 us (11%)
  between operations  0.65 us (2%)
    pallas_call x1, Pallas kernels, shards(): pl.pallas_call(functools.partial(kernel, n_dp, n_mp), out_shape=(jax.Shap...  30.3 us
    unnamed x7, local copies, waits for them, and re-layouts  3.75 us

profile of v2, /device:TPU:1, one launch (start us, length us, event | category | flops | bytes accessed | tf_op | source)
XLA Modules:
  0.0 34.7 jit_solution(7599883420965099530)
XLA Ops:
  0.6 30.3 %shard_map.85 = (bf16[8,32,512]{2,1,0:T(8,128)(2,1)}, bf16[512,512]{1,0:T(8,128)(2,1)}, bf16[512,512]{1,0:T(8,128)(2,1)}) custom-call(s32[1,8]{1,0:T(1,128)} %owners.1, bf16[8,32,512]{2,1,0:T(8,128)(2,1)} %bitcast.14, f32[512,512]{1,0:T(8,128)} %bitcast.8, f32[512,512]{1,0:T(8,128)} %bitcast.9, bf16[512,512]{1,0:T(8,128)(2,1)} %bitcast.12, ...), custom_call_target="tpu_custom_call" | custom-call | tf_op jit(solution)/shard_map/pallas_call | solution.py:280
  30.9 0.0 copy-start.1
  31.0 1.7 %copy.12 = bf16[1,8,32,512]{3,2,1,0:T(8,128)(2,1)} copy(bf16[1,8,32,512]{3,2,1,0:T(8,128)(2,1)} %bitcast.15) | data formatting | bytes 524288
  32.7 0.0 copy-done.1
  32.7 0.0 copy-start
  32.7 0.8 %copy.13 = bf16[1,1,512,512]{3,2,1,0:T(8,128)(2,1)} copy(bf16[1,1,512,512]{3,2,1,0:T(8,128)(2,1)S(1)} %bitcast.11) | data formatting | bytes 1048576
  33.5 0.4 %copy-done = bf16[512,512]{1,0:T(8,128)(2,1)S(1)} copy-done((bf16[512,512]{1,0:T(8,128)(2,1)S(1)}, bf16[512,512]{1,0:T(8,128)(2,1)}, u32[]{:S(2)}) %copy-start) | copy-done | bytes 524312
  33.9 0.8 %copy.14 = bf16[1,1,512,512]{3,2,1,0:T(8,128)(2,1)} copy(bf16[1,1,512,512]{3,2,1,0:T(8,128)(2,1)S(1)} %bitcast.10) | data formatting | bytes 1048576
Async XLA Ops:
  30.9 1.7 %copy-start.1 = (bf16[512,512]{1,0:T(8,128)(2,1)S(1)}, bf16[512,512]{1,0:T(8,128)(2,1)}, u32[]{:S(2)}) copy-start(bf16[512,512]{1,0:T(8,128)(2,1)} %get-tuple-element.7) | copy-start | bytes 1572868
  32.7 1.2 %copy-start = (bf16[512,512]{1,0:T(8,128)(2,1)S(1)}, bf16[512,512]{1,0:T(8,128)(2,1)}, u32[]{:S(2)}) copy-start(bf16[512,512]{1,0:T(8,128)(2,1)} %get-tuple-element.8) | copy-start | bytes 1572868

commit v3 on v2

--- a/solution.py
+++ b/solution.py
@@ -233,15 +233,15 @@
     loads[3].wait()
     refresh(lstat, mm(block, block, ((1,), (1,))), lout)
 
+    loads[4].wait()
+    refresh(rstat, mm(block, block, ((0,), (0,))), rout)
+
     each(1, n_dp, lambda i: norm_from(lax.rem(me + i, n_dp)).wait_recv())
     row_out[...] = lax.fori_loop(
         0, nb, lambda j, a: jnp.where(lane == j, norm_in[owners[0, j]], a), jnp.zeros((2, 128), jnp.float32)
     )
     each(1, n_mp, lambda i: row_to(lax.rem(mine + i, n_mp)).start())
     row_in[mine] = row_out[...]
-
-    loads[4].wait()
-    refresh(rstat, mm(block, block, ((0,), (0,))), rout)
 
     each(first, half, pass_dir)
 
@@ -267,6 +267,24 @@
     each(first, half, lambda d: dir_on(behind(d)).wait_send())
     each(1, n_dp, lambda i: norm_to(lax.rem(me + i, n_dp)).wait_send())
     each(1, n_mp, lambda i: row_to(lax.rem(mine + i, n_mp)).wait_send())
+
+
+def settle(update_in, left_in, right_in, update, left, right, a, b, c, sems):
+    ins = [
+        pltpu.make_async_copy(src, dst, sems.at[i])
+        for i, (src, dst) in enumerate([(left_in, b), (right_in, c), (update_in, a)])
+    ]
+    outs = [
+        pltpu.make_async_copy(src, dst, sems.at[3 + i])
+        for i, (src, dst) in enumerate([(b, left), (c, right), (a, update)])
+    ]
+    for copy in ins:
+        copy.start()
+    for arrives, leaves in zip(ins, outs):
+        arrives.wait()
+        leaves.start()
+    for copy in outs:
+        copy.wait()
 
 
 def shards(n_dp, n_mp, gradient, owners, left_stats, right_stats, left_roots_old, right_roots_old):
@@ -305,6 +323,18 @@
             collective_id=0, has_side_effects=True
         ),
     )(owners, gradient[0], left_stats[0, 0], right_stats[0, 0], left_roots_old[0, 0], right_roots_old[0, 0])
+    update, left, right = pl.pallas_call(
+        settle,
+        out_shape=(jax.ShapeDtypeStruct((nb, rows, width), bf16), square, square),
+        in_specs=[hbm] * 3,
+        out_specs=(hbm,) * 3,
+        scratch_shapes=[
+            pltpu.VMEM((nb, rows, width), bf16),
+            pltpu.VMEM((width, width), bf16),
+            pltpu.VMEM((width, width), bf16),
+            dma((6,)),
+        ],
+    )(update, left, right)
     return update[None], left[None, None], right[None, None]
 
 

time: 34.9 us -> 31.2 us (0.89)
  the two profiles are of different devices: /device:TPU:1 before, /device:TPU:25 now
where the time goes in v3:
time: 31.2 us; the launch traced here: 31.1 us
  Pallas kernels  30.5 us (98%)
  between operations  0.64 us (2%)
    pallas_call x1, Pallas kernels, shards(): pl.pallas_call(functools.partial(kernel, n_dp, n_mp), out_shape=(jax.Shap...  28.3 us
    pallas_call x1, Pallas kernels, shards(): pl.pallas_call(settle, out_shape=(jax.ShapeDtypeStruct((nb, rows, width),...  2.14 us

profile of v3, /device:TPU:25, one launch (start us, length us, event | category | flops | bytes accessed | tf_op | source)
XLA Modules:
  0.0 31.1 jit_solution(2606851190379201035)
XLA Ops:
  0.6 28.3 %shard_map.85 = (bf16[8,32,512]{2,1,0:T(8,128)(2,1)}, bf16[512,512]{1,0:T(8,128)(2,1)}, bf16[512,512]{1,0:T(8,128)(2,1)}) custom-call(s32[1,8]{1,0:T(1,128)} %owners.1, bf16[8,32,512]{2,1,0:T(8,128)(2,1)} %bitcast.12, f32[512,512]{1,0:T(8,128)} %bitcast.8, f32[512,512]{1,0:T(8,128)} %bitcast.9, bf16[512,512]{1,0:T(8,128)(2,1)} %bitcast.10, ...), custom_call_target="tpu_custom_call" | custom-call | tf_op jit(solution)/shard_map/pallas_call | solution.py:298
  29.0 2.1 %shard_map.86 = (bf16[8,32,512]{2,1,0:T(8,128)(2,1)}, bf16[512,512]{1,0:T(8,128)(2,1)}, bf16[512,512]{1,0:T(8,128)(2,1)}) custom-call(bf16[8,32,512]{2,1,0:T(8,128)(2,1)} %get-tuple-element.9.update_in, bf16[512,512]{1,0:T(8,128)(2,1)} %get-tuple-element.10.left_in, bf16[512,512]{1,0:T(8,128)(2,1)} %get-tuple-element.11.right_in), custom_call_target="tpu_custom_call" | custom-call | tf_op jit(solution)/shard_map/pallas_call | solution.py:326

commit v4 on v3

--- a/solution.py
+++ b/solution.py
@@ -47,11 +47,11 @@
 def kernel(
     n_dp, n_mp,
     owners, grad_hbm, lstat_hbm, rstat_hbm, lroot_hbm, rroot_hbm,
-    upd, lout, rout,
-    grad, lstat, rstat, roots,
+    update_hbm, lout_hbm, rout_hbm,
+    upd, lout, rout, grad, lstat, rstat, roots,
     stay, go, outgoing, arrived, direction, returned,
     norm_out, norm_in, row_out, row_in,
-    load_sem, swap_sem, gs_sem, gr_sem, gf_sem, ds_sem, dr_sem, df_sem,
+    load_sem, store_sem, swap_sem, gs_sem, gr_sem, gf_sem, ds_sem, dr_sem, df_sem,
     ns_sem, nr_sem, rs_sem, rr_sem,
 ):
     me = lax.axis_index("dp")
@@ -204,12 +204,12 @@
     each(0, half, lambda d: grad_on(across(d)).wait_recv())
 
     block = joined(arrived[...])
+    block32 = block.astype(jnp.float32)
+    g_sum = jnp.sum(block32 * block32, keepdims=True)
     shaded = mm(block, roots[1 - busy, 1]).astype(jnp.bfloat16)
     moved = mm(roots[1 - busy, 0], shaded).astype(jnp.bfloat16)
     direction[...] = split(moved)
-    block32 = block.astype(jnp.float32)
     moved32 = moved.astype(jnp.float32)
-    g_sum = jnp.sum(block32 * block32, keepdims=True)
     d_sum = jnp.sum(moved32 * moved32, keepdims=True)
     sub = lax.broadcasted_iota(jnp.int32, (2, 128), 0)
     lane = lax.broadcasted_iota(jnp.int32, (2, 128), 1)
@@ -232,9 +232,13 @@
 
     loads[3].wait()
     refresh(lstat, mm(block, block, ((1,), (1,))), lout)
+    lcopy = pltpu.make_async_copy(lout, lout_hbm, store_sem.at[0])
+    lcopy.start()
 
     loads[4].wait()
     refresh(rstat, mm(block, block, ((0,), (0,))), rout)
+    rcopy = pltpu.make_async_copy(rout, rout_hbm, store_sem.at[1])
+    rcopy.start()
 
     each(1, n_dp, lambda i: norm_from(lax.rem(me + i, n_dp)).wait_recv())
     row_out[...] = lax.fori_loop(
@@ -257,6 +261,8 @@
         upd[j] = (factor * returned[owners[0, j]].astype(jnp.float32)).astype(jnp.bfloat16)
 
     each(0, nb, finish)
+    ucopy = pltpu.make_async_copy(upd, update_hbm, store_sem.at[2])
+    ucopy.start()
 
     swap.wait_send()
     swap_r.wait_send()
@@ -267,6 +273,9 @@
     each(first, half, lambda d: dir_on(behind(d)).wait_send())
     each(1, n_dp, lambda i: norm_to(lax.rem(me + i, n_dp)).wait_send())
     each(1, n_mp, lambda i: row_to(lax.rem(mine + i, n_mp)).wait_send())
+    lcopy.wait()
+    rcopy.wait()
+    ucopy.wait()
 
 
 def settle(update_in, left_in, right_in, update, left, right, a, b, c, sems):
@@ -291,7 +300,6 @@
     _, nb, rows, width = gradient.shape
     half = n_dp // 2
     hbm = pl.BlockSpec(memory_space=pltpu.HBM)
-    vmem = pl.BlockSpec(memory_space=pltpu.VMEM)
     bf16, f32 = jnp.bfloat16, jnp.float32
     dma = pltpu.SemaphoreType.DMA
     square = jax.ShapeDtypeStruct((width, width), bf16)
@@ -299,8 +307,11 @@
         functools.partial(kernel, n_dp, n_mp),
         out_shape=(jax.ShapeDtypeStruct((nb, rows, width), bf16), square, square),
         in_specs=[pl.BlockSpec(memory_space=pltpu.SMEM)] + [hbm] * 5,
-        out_specs=(vmem,) * 3,
+        out_specs=(hbm,) * 3,
         scratch_shapes=[
+            pltpu.VMEM((nb, rows, width), bf16),
+            pltpu.VMEM((width, width), bf16),
+            pltpu.VMEM((width, width), bf16),
             pltpu.VMEM((nb, rows, width), bf16),
             pltpu.VMEM((width, width), f32),
             pltpu.VMEM((width, width), f32),
@@ -315,7 +326,7 @@
             pltpu.VMEM((n_dp, 2, 128), f32),
             pltpu.VMEM((2, 128), f32),
             pltpu.VMEM((n_mp, 2, 128), f32),
-            dma((5,)), dma((6,)),
+            dma((5,)), dma((3,)), dma((6,)),
             *[dma((n_dp,)) for _ in range(8)],
             dma((n_mp,)), dma((n_mp,)),
         ],

time: 31.2 us -> 30.4 us (0.974)
  Pallas kernels: 30.5 us -> 29.6 us
    pallas_call x1, Pallas kernels: 28.3 us -> 27.5 us  [shards(): pl.pallas_call(functools.partial(kernel, n_dp, n_mp), out_shape=(jax.Shap...]
where the time goes in v4:
time: 30.4 us; the launch traced here: 30.3 us
  Pallas kernels  29.6 us (97%)
  between operations  0.64 us (2%)
    pallas_call x1, Pallas kernels, shards(): pl.pallas_call(functools.partial(kernel, n_dp, n_mp), out_shape=(jax.Shap...  27.5 us
    pallas_call x1, Pallas kernels, shards(): pl.pallas_call(settle, out_shape=(jax.ShapeDtypeStruct((nb, rows, width),...  2.14 us

profile of v4, /device:TPU:25, one launch (start us, length us, event | category | flops | bytes accessed | tf_op | source)
XLA Modules:
  0.0 30.3 jit_solution(15895400230706332865)
XLA Ops:
  0.6 27.5 %shard_map.85 = (bf16[8,32,512]{2,1,0:T(8,128)(2,1)}, bf16[512,512]{1,0:T(8,128)(2,1)}, bf16[512,512]{1,0:T(8,128)(2,1)}) custom-call(s32[1,8]{1,0:T(1,128)} %owners.1, bf16[8,32,512]{2,1,0:T(8,128)(2,1)} %bitcast.12, f32[512,512]{1,0:T(8,128)} %bitcast.8, f32[512,512]{1,0:T(8,128)} %bitcast.9, bf16[512,512]{1,0:T(8,128)(2,1)} %bitcast.10, ...), custom_call_target="tpu_custom_call" | custom-call | tf_op jit(solution)/shard_map/pallas_call | solution.py:306
  28.1 2.1 %shard_map.86 = (bf16[8,32,512]{2,1,0:T(8,128)(2,1)}, bf16[512,512]{1,0:T(8,128)(2,1)}, bf16[512,512]{1,0:T(8,128)(2,1)}) custom-call(bf16[8,32,512]{2,1,0:T(8,128)(2,1)} %get-tuple-element.9.update_in, bf16[512,512]{1,0:T(8,128)(2,1)} %get-tuple-element.10.left_in, bf16[512,512]{1,0:T(8,128)(2,1)} %get-tuple-element.11.right_in), custom_call_target="tpu_custom_call" | custom-call | tf_op jit(solution)/shard_map/pallas_call | solution.py:337
